TPU v7x, 32 devices: a whole 2x2x4 slice. The times are simulated.
32 devices in a mesh: grp: 2 (over x), col: 16 (over z, y, core).
Axes of the slice: x: 2, y: 2, z: 4, core: 2. Of those that a mesh axis runs over, the one named last changes fastest.
Arguments:
- database: int32 [256, 4096], P('col', 'grp'), parts along dimension 1, may hold values from 0 to 255
- queries: int32 [16, 256], P('grp', 'col'), parts along dimension 0, may hold values from -2147483648 to 2147483646
- key_rows: int32 [16, 8192], P('grp', 'col'), parts along dimension 0, may hold values from -2147483648 to 2147483646
- hint: int32 [4, 1024], P('grp'), parts along dimension 0, may hold values from -2147483648 to 2147483646
- assignment: int32 [32], P('grp'), parts along dimension 0, may hold values from 0 to 15, each once
Outputs:
- packed: float32 [32, 2, 1024], P(('grp', 'col')), parts along dimension 0
There are 2 independent parts, one for each index of `grp`. A program takes and returns all parts, laid end to end along the dimension named above; each array names one. Nothing has to cross between parts.
Inputs may be any that keep to these rules, and one draw needn't show every extreme that they name: `assignment`: every unit appears in exactly one slot.
All inputs are finite; a program needn't handle non-finite values.
Results may differ from a plain program's by a relative error of at most 0.0003.
Values sent between devices are 32-bit elements; how exact they have to be, the bound alone decides.
A program may use at most 128 MiB of HBM per device.

v0:
```python
import jax
import jax.numpy as jnp
from jax import lax
from jax.sharding import PartitionSpec as P

LEVELS = 2
DIGITS = 2


def automorph(polynomial, galois):
    cycle_width = polynomial.shape[0]
    inverse = pow(galois, -1, 2 * cycle_width)
    source = jnp.arange(cycle_width, dtype=jnp.int32) * inverse % (2 * cycle_width)
    picked = jnp.take(polynomial, source % cycle_width, axis=0)
    return jnp.where(source < cycle_width, picked, -picked)


def toeplitz(key_poly):
    cycle_width = key_poly.shape[0]
    shifted = jnp.concatenate([-key_poly[1:], key_poly, -key_poly[:1]])
    tiled_rows = jnp.tile(shifted, cycle_width)[: cycle_width * (2 * cycle_width - 1)]
    return tiled_rows.reshape(cycle_width, 2 * cycle_width - 1)[
        :, cycle_width - 1 : 2 * cycle_width - 1
    ]


def switch_section(mask_poly, value_poly, section_keys, galois):
    cycle_width = mask_poly.shape[0]
    rotated_mask = automorph(mask_poly, galois)
    rotated_value = automorph(value_poly, galois)
    switched = jnp.zeros((2 * cycle_width,), jnp.int32)
    for digit_index in range(section_keys.shape[0]):
        digit_row = jnp.bitwise_and(jnp.right_shift(rotated_mask, 16 * digit_index), 65535)
        matrix = jnp.concatenate(
            [toeplitz(section_keys[digit_index, 0]), toeplitz(section_keys[digit_index, 1])], axis=1
        )
        switched = (
            switched + jnp.dot(digit_row[None, :], matrix, preferred_element_type=jnp.int32)[0]
        )
    return (mask_poly + switched[:cycle_width], value_poly + rotated_value + switched[cycle_width:])


def pack_unit(mask_poly, value_poly, key_row):
    cycle_width = mask_poly.shape[0]
    section_table = key_row.reshape(LEVELS, DIGITS, 2, cycle_width)
    for section_index in range(LEVELS):
        galois = cycle_width // 2**section_index + 1
        mask_poly, value_poly = switch_section(
            mask_poly, value_poly, section_table[section_index], galois
        )
    return jnp.stack([mask_poly, value_poly])


def split_words(words):
    lower_half = jnp.bitwise_and(words, 65535).astype(jnp.float32)
    upper_half = jnp.bitwise_and(jnp.right_shift(words, 16), 65535).astype(jnp.float32)
    return (lower_half, upper_half)


def join_words(lower_half, upper_half):
    return lower_half.astype(jnp.int32) + jnp.left_shift(upper_half.astype(jnp.int32), 16)


def on_device(database, queries, key_rows, hint, assignment):
    cycle_width = hint.shape[1]
    poly_count = hint.shape[0]
    slot_count = assignment.shape[0] // lax.axis_size("col")
    key_table = lax.all_gather(key_rows, "col", axis=1, tiled=True)
    partial_value = jnp.dot(queries, database, preferred_element_type=jnp.int32)
    owned_slots = lax.dynamic_slice_in_dim(
        assignment, lax.axis_index("col") * slot_count, slot_count
    )
    lower_half, upper_half = split_words(partial_value)
    lower_sum, upper_sum = lax.psum((lower_half, upper_half), "col")
    summed = join_words(lower_sum, upper_sum)
    value_rows = jnp.take(summed.reshape(-1, cycle_width), owned_slots, axis=0)

    def pack_one(inputs):
        unit_index, value_poly = inputs
        client = unit_index // poly_count
        poly_index = unit_index % poly_count
        mask_poly = lax.dynamic_index_in_dim(hint, poly_index, 0, keepdims=False)
        key_row = lax.dynamic_index_in_dim(key_table, client, 0, keepdims=False)
        return pack_unit(mask_poly, value_poly, key_row)

    packed_words = lax.map(pack_one, (owned_slots, value_rows))
    return packed_words.astype(jnp.float32) * 2.0 ** (-32)


def solution(mesh):
    placed = (P("col", "grp"), P("grp", "col"), P("grp", "col"), P("grp", None), P("grp"))
    return jax.shard_map(
        on_device,
        mesh=mesh,
        in_specs=placed,
        out_specs=P(("grp", "col"), None, None),
        check_vma=False,
    )
```

profile of v0, /device:TPU:0, one launch (start us, length us, event | category | flops | bytes accessed | tf_op | source)
XLA Modules:
  0.0 325.9 jit_solution(6749545963673076256)
XLA Ops:
  12.9 24.2 %all_gather.3 = s32[8,8192]{1,0:T(8,128)S(1)} all-gather(s32[8,512]{1,0:T(8,128)} %param.9), channel_id=1, replica_groups=mesh['grp'=2,'col'=16] {'col'}, dimensions={1}, use_global_device_ids=true | all-gather | bytes 278528 | tf_op jit(solution)/shard_map/all_gather | solution.py:68
  46.2 12.3 %reshape.150 = s32[1024,2047]{1,0:T(8,128)} reshape(s32[2096128]{0:T(1024)} %slice.292) | data formatting | bytes 16769024 | tf_op jit(solution)/shard_map/while/body/eval_jaxpr/reshape | solution.py:22
  58.5 5.5 %slice.293 = s32[1024,1024]{1,0:T(8,128)} slice(s32[1024,2047]{1,0:T(8,128)} %reshape.150), slice={[0:1024], [1023:2047]} | slice | bytes 8388608 | tf_op jit(solution)/shard_map/while/body/eval_jaxpr/slice | solution.py:22
  71.6 12.3 %reshape.151 = s32[1024,2047]{1,0:T(8,128)} reshape(s32[2096128]{0:T(1024)} %slice.297) | data formatting | bytes 16769024 | tf_op jit(solution)/shard_map/while/body/eval_jaxpr/reshape | solution.py:22
  83.9 5.5 %slice.298 = s32[1024,1024]{1,0:T(8,128)} slice(s32[1024,2047]{1,0:T(8,128)} %reshape.151), slice={[0:1024], [1023:2047]} | slice | bytes 8388608 | tf_op jit(solution)/shard_map/while/body/eval_jaxpr/slice | solution.py:22
  101.7 12.3 %reshape.148 = s32[1024,2047]{1,0:T(8,128)} reshape(s32[2096128]{0:T(1024)} %slice.282) | data formatting | bytes 16769024 | tf_op jit(solution)/shard_map/while/body/eval_jaxpr/reshape | solution.py:22
  114.0 5.4 %slice.283 = s32[1024,1024]{1,0:T(8,128)} slice(s32[1024,2047]{1,0:T(8,128)} %reshape.148), slice={[0:1024], [1023:2047]} | slice | bytes 8388608 | tf_op jit(solution)/shard_map/while/body/eval_jaxpr/slice | solution.py:22
  126.9 12.3 %reshape.149 = s32[1024,2047]{1,0:T(8,128)} reshape(s32[2096128]{0:T(1024)} %slice.287) | data formatting | bytes 16769024 | tf_op jit(solution)/shard_map/while/body/eval_jaxpr/reshape | solution.py:22
  139.2 5.4 %slice.288 = s32[1024,1024]{1,0:T(8,128)} slice(s32[1024,2047]{1,0:T(8,128)} %reshape.149), slice={[0:1024], [1023:2047]} | slice | bytes 8388608 | tf_op jit(solution)/shard_map/while/body/eval_jaxpr/slice | solution.py:22
  166.8 7.0 %fusion.4 = s32[1,2048]{1,0:T(1,128)S(1)} fusion(s32[1024,1]{0,1:T(1,128)S(1)} %bitcast.88, s32[1024,1024]{1,0:T(8,128)S(1)} %copy-done.3, s32[1024,1024]{1,0:T(8,128)S(1)} %copy-done.2), kind=kOutput, calls=%fused_computation.8 | convolution fusion | flops 6291456 | bytes 8400896 | tf_op jit(solution)/shard_map/while/body/eval_jaxpr/dot_general | solution.py:38
  173.8 6.8 %fusion = s32[1,2048]{1,0:T(1,128)S(1)} fusion(s32[1024,1]{0,1:T(1,128)S(1)} %bitcast.87, s32[1024,1024]{1,0:T(8,128)S(1)} %copy-done.7, s32[1024,1024]{1,0:T(8,128)S(1)} %copy-done.4), kind=kOutput, calls=%fused_computation.4 | convolution fusion | flops 6291456 | bytes 8400896 | tf_op jit(solution)/shard_map/while/body/eval_jaxpr/dot_general | solution.py:38
  188.5 12.3 %reshape.154 = s32[1024,2047]{1,0:T(8,128)} reshape(s32[2096128]{0:T(1024)} %slice.313) | data formatting | bytes 16769024 | tf_op jit(solution)/shard_map/while/body/eval_jaxpr/reshape | solution.py:22
  200.8 5.5 %slice.314 = s32[1024,1024]{1,0:T(8,128)} slice(s32[1024,2047]{1,0:T(8,128)} %reshape.154), slice={[0:1024], [1023:2047]} | slice | bytes 8388608 | tf_op jit(solution)/shard_map/while/body/eval_jaxpr/slice | solution.py:22
  206.4 5.4 %copy.13 = s32[128,16,8,128]{3,1,2,0:T(8,128)S(1)} copy(s32[128,16,8,128]{3,2,1,0:T(8,128)} %broadcast_bitcast_fusion) | data formatting | bytes 16777216
  215.4 12.3 %reshape.155 = s32[1024,2047]{1,0:T(8,128)} reshape(s32[2096128]{0:T(1024)} %slice.318) | data formatting | bytes 16769024 | tf_op jit(solution)/shard_map/while/body/eval_jaxpr/reshape | solution.py:22
  227.8 5.5 %slice.319 = s32[1024,1024]{1,0:T(8,128)} slice(s32[1024,2047]{1,0:T(8,128)} %reshape.155), slice={[0:1024], [1023:2047]} | slice | bytes 8388608 | tf_op jit(solution)/shard_map/while/body/eval_jaxpr/slice | solution.py:22
  233.2 5.4 %copy.10 = s32[128,16,8,128]{3,1,2,0:T(8,128)S(1)} copy(s32[128,16,8,128]{3,2,1,0:T(8,128)} %broadcast_bitcast_fusion.3) | data formatting | bytes 16777216
  242.3 12.3 %reshape.152 = s32[1024,2047]{1,0:T(8,128)} reshape(s32[2096128]{0:T(1024)} %slice.303) | data formatting | bytes 16769024 | tf_op jit(solution)/shard_map/while/body/eval_jaxpr/reshape | solution.py:22
  254.6 5.4 %slice.304 = s32[1024,1024]{1,0:T(8,128)} slice(s32[1024,2047]{1,0:T(8,128)} %reshape.152), slice={[0:1024], [1023:2047]} | slice | bytes 8388608 | tf_op jit(solution)/shard_map/while/body/eval_jaxpr/slice | solution.py:22
  260.0 5.4 %copy.11 = s32[128,16,8,128]{3,1,2,0:T(8,128)S(1)} copy(s32[128,16,8,128]{3,2,1,0:T(8,128)} %broadcast_bitcast_fusion.2) | data formatting | bytes 16777216
  269.2 12.3 %reshape.153 = s32[1024,2047]{1,0:T(8,128)} reshape(s32[2096128]{0:T(1024)} %slice.308) | data formatting | bytes 16769024 | tf_op jit(solution)/shard_map/while/body/eval_jaxpr/reshape | solution.py:22
  281.5 5.4 %slice.309 = s32[1024,1024]{1,0:T(8,128)} slice(s32[1024,2047]{1,0:T(8,128)} %reshape.153), slice={[0:1024], [1023:2047]} | slice | bytes 8388608 | tf_op jit(solution)/shard_map/while/body/eval_jaxpr/slice | solution.py:22
  301.6 9.5 %fusion.12 = s32[1,2048]{1,0:T(1,128)S(1)} fusion(s32[1024,1]{0,1:T(1,128)S(1)} %bitcast.90, s32[1024,1024]{1,0:T(8,128)} %slice.319, s32[1024,1024]{1,0:T(8,128)} %slice.314), kind=kOutput, calls=%fused_computation.16 | convolution fusion | flops 6291456 | bytes 8400896 | tf_op jit(solution)/shard_map/while/body/eval_jaxpr/dot_general | solution.py:38
  311.1 6.8 %fusion.8 = s32[1,2048]{1,0:T(1,128)S(1)} fusion(s32[1024,1]{0,1:T(1,128)S(1)} %bitcast.89, s32[1024,1024]{1,0:T(8,128)S(1)} %copy-done.6, s32[1024,1024]{1,0:T(8,128)S(1)} %copy-done.5), kind=kOutput, calls=%fused_computation.12 | convolution fusion | flops 6291456 | bytes 8400896 | tf_op jit(solution)/shard_map/while/body/eval_jaxpr/dot_general | solution.py:38
  (82 shorter events, 89.5 us)
Async XLA Ops:
  6.5 0.9 copy-start
  6.5 280.4 %all-reduce.3.cloned.1.call-start = ((), (), s32[]{:S(2)}) async-start(), calls=%async_computation | async-start | bytes 262144 | tf_op jit(solution)/shard_map/psum | solution.py:74
  83.9 5.5 %copy-start.8 = (s32[2,1024]{1,0:T(2,128)S(1)}, s32[2,1024]{1,0:T(2,128)}, u32[]{:S(2)}) copy-start(s32[2,1024]{1,0:T(2,128)} %param.10) | copy-start | bytes 24580
  160.3 5.3 %copy-start.2 = (s32[1024,1024]{1,0:T(8,128)S(1)}, s32[1024,1024]{1,0:T(8,128)}, u32[]{:S(2)}) copy-start(s32[1024,1024]{1,0:T(8,128)} %slice.293) | copy-start | bytes 12582916
  160.3 6.5 %copy-start.3 = (s32[1024,1024]{1,0:T(8,128)S(1)}, s32[1024,1024]{1,0:T(8,128)}, u32[]{:S(2)}) copy-start(s32[1024,1024]{1,0:T(8,128)} %slice.298) | copy-start | bytes 12582916
  160.3 13.5 %copy-start.4 = (s32[1024,1024]{1,0:T(8,128)S(1)}, s32[1024,1024]{1,0:T(8,128)}, u32[]{:S(2)}) copy-start(s32[1024,1024]{1,0:T(8,128)} %slice.283) | copy-start | bytes 12582916
  160.3 13.5 %copy-start.7 = (s32[1024,1024]{1,0:T(8,128)S(1)}, s32[1024,1024]{1,0:T(8,128)}, u32[]{:S(2)}) copy-start(s32[1024,1024]{1,0:T(8,128)} %slice.288) | copy-start | bytes 12582916
  166.8 15.7 %slice-start = ((s8[8388608]{0:T(1024)(128)(4,1)}), s8[4194304]{0:T(1024)(128)(4,1)S(1)}, s32[]{:S(2)}) async-start(s8[8388608]{0:T(1024)(128)(4,1)} %bitcast.73), calls=%async_computation.1 | async-start | bytes 8388608
  173.8 8.7 %slice-start.1 = ((s8[8388608]{0:T(1024)(128)(4,1)}), s8[4194304]{0:T(1024)(128)(4,1)S(1)}, s32[]{:S(2)}) async-start(s8[8388608]{0:T(1024)(128)(4,1)} %bitcast.73), calls=%async_computation.2 | async-start | bytes 8388608
  301.5 9.6 %copy-start.5 = (s32[1024,1024]{1,0:T(8,128)S(1)}, s32[1024,1024]{1,0:T(8,128)}, u32[]{:S(2)}) copy-start(s32[1024,1024]{1,0:T(8,128)} %slice.304) | copy-start | bytes 12582916
  301.6 9.6 %copy-start.6 = (s32[1024,1024]{1,0:T(8,128)S(1)}, s32[1024,1024]{1,0:T(8,128)}, u32[]{:S(2)}) copy-start(s32[1024,1024]{1,0:T(8,128)} %slice.309) | copy-start | bytes 12582916
  301.6 17.0 %copy-start.1 = (s32[16,2048]{1,0:T(8,128)S(1)}, s32[16,2048]{1,0:T(8,128)}, u32[]{:S(2)}) copy-start(s32[16,2048]{1,0:T(8,128)} %param.7) | copy-start | bytes 393220
Sparse Core Ops, SparseCore 0:
  10.9 91.1 all-reduce.2
where the time goes:
time: 330 us; the launch traced here: 326 us
  local copies, waits for them, and re-layouts  244 us (74%)
  matrix products  31.6 us (10%)
  blocking collectives  24.2 us (7%)
  between operations  23.8 us (7%)
    reshape x8, local copies, waits for them, and re-layouts, toeplitz(): tiled_rows.reshape(cycle_width, 2 * cycle_width - 1)  98.5 us
    unnamed x38, local copies, waits for them, and re-layouts  51 us
    slice x8, local copies, waits for them, and re-layouts, toeplitz(): tiled_rows.reshape(cycle_width, 2 * cycle_width - 1)  43.7 us
    dot_general x4, matrix products, switch_section(): jnp.dot(digit_row[None, :], matrix, preferred_element_type=jnp.int32)[0]  30 us
    slice x8, local copies, waits for them, and re-layouts, toeplitz(): jnp.tile(shifted, cycle_width)[:cycle_width * (2 * cycle_width - 1)]  29.8 us
    all_gather x1, blocking collectives, on_device(): key_table = lax.all_gather(key_rows, 'col', axis=1, tiled=True)  24.2 us
    gather x4, local copies, waits for them, and re-layouts, automorph(): picked = jnp.take(polynomial, source % cycle_width, axis=0)  18.1 us
  transfers between devices with their start and end apart: 1, of which 0 were waited for; matrix products, arithmetic and copies ran while one was open for 74% of the time, Pallas kernels for 0%

commit v1 on v0

--- a/solution.py
+++ b/solution.py
@@ -65,7 +65,7 @@
     cycle_width = hint.shape[1]
     poly_count = hint.shape[0]
     slot_count = assignment.shape[0] // lax.axis_size("col")
-    key_table = lax.all_gather(key_rows, "col", axis=1, tiled=True)
+    key_table = jnp.concatenate(lax.all_gather(key_rows, "col"), axis=1)
     partial_value = jnp.dot(queries, database, preferred_element_type=jnp.int32)
     owned_slots = lax.dynamic_slice_in_dim(
         assignment, lax.axis_index("col") * slot_count, slot_count

time: 330 us -> 330 us (level)
  no operation moved by 1% of the time
where the time goes in v1:
time: 330 us; the launch traced here: 326 us
  local copies, waits for them, and re-layouts  244 us (74%)
  matrix products  31.6 us (10%)
  blocking collectives  24.2 us (7%)
  between operations  23.8 us (7%)
    reshape x8, local copies, waits for them, and re-layouts, toeplitz(): tiled_rows.reshape(cycle_width, 2 * cycle_width - 1)  98.5 us
    unnamed x38, local copies, waits for them, and re-layouts  51 us
    slice x8, local copies, waits for them, and re-layouts, toeplitz(): tiled_rows.reshape(cycle_width, 2 * cycle_width - 1)  43.7 us
    dot_general x4, matrix products, switch_section(): jnp.dot(digit_row[None, :], matrix, preferred_element_type=jnp.int32)[0]  30 us
    slice x8, local copies, waits for them, and re-layouts, toeplitz(): jnp.tile(shifted, cycle_width)[:cycle_width * (2 * cycle_width - 1)]  29.8 us
    all_gather x1, blocking collectives, on_device(): key_table = jnp.concatenate(lax.all_gather(key_rows, 'col'), axis=1)  24.2 us
    gather x4, local copies, waits for them, and re-layouts, automorph(): picked = jnp.take(polynomial, source % cycle_width, axis=0)  18.1 us
  transfers between devices with their start and end apart: 1, of which 0 were waited for; matrix products, arithmetic and copies ran while one was open for 74% of the time, Pallas kernels for 0%

profile of v1, /device:TPU:0, one launch (start us, length us, event | category | flops | bytes accessed | tf_op | source)
XLA Modules:
  0.0 325.9 jit_solution(15908655947112434860)
XLA Ops:
  12.9 24.2 %all-gather = s32[128,512]{1,0:T(8,128)S(1)} all-gather(s32[8,512]{1,0:T(8,128)} %param.9), channel_id=2, replica_groups=mesh['grp'=2,'col'=16] {'col'}, dimensions={0}, use_global_device_ids=true | all-gather | bytes 278528 | tf_op jit(solution)/shard_map/all_gather | solution.py:68
  46.2 12.3 %reshape.158 = s32[1024,2047]{1,0:T(8,128)} reshape(s32[2096128]{0:T(1024)} %slice.292) | data formatting | bytes 16769024 | tf_op jit(solution)/shard_map/while/body/eval_jaxpr/reshape | solution.py:22
  58.5 5.5 %slice.293 = s32[1024,1024]{1,0:T(8,128)} slice(s32[1024,2047]{1,0:T(8,128)} %reshape.158), slice={[0:1024], [1023:2047]} | slice | bytes 8388608 | tf_op jit(solution)/shard_map/while/body/eval_jaxpr/slice | solution.py:22
  71.6 12.3 %reshape.159 = s32[1024,2047]{1,0:T(8,128)} reshape(s32[2096128]{0:T(1024)} %slice.297) | data formatting | bytes 16769024 | tf_op jit(solution)/shard_map/while/body/eval_jaxpr/reshape | solution.py:22
  83.9 5.5 %slice.298 = s32[1024,1024]{1,0:T(8,128)} slice(s32[1024,2047]{1,0:T(8,128)} %reshape.159), slice={[0:1024], [1023:2047]} | slice | bytes 8388608 | tf_op jit(solution)/shard_map/while/body/eval_jaxpr/slice | solution.py:22
  101.7 12.3 %reshape.156 = s32[1024,2047]{1,0:T(8,128)} reshape(s32[2096128]{0:T(1024)} %slice.282) | data formatting | bytes 16769024 | tf_op jit(solution)/shard_map/while/body/eval_jaxpr/reshape | solution.py:22
  114.0 5.4 %slice.283 = s32[1024,1024]{1,0:T(8,128)} slice(s32[1024,2047]{1,0:T(8,128)} %reshape.156), slice={[0:1024], [1023:2047]} | slice | bytes 8388608 | tf_op jit(solution)/shard_map/while/body/eval_jaxpr/slice | solution.py:22
  126.9 12.3 %reshape.157 = s32[1024,2047]{1,0:T(8,128)} reshape(s32[2096128]{0:T(1024)} %slice.287) | data formatting | bytes 16769024 | tf_op jit(solution)/shard_map/while/body/eval_jaxpr/reshape | solution.py:22
  139.2 5.4 %slice.288 = s32[1024,1024]{1,0:T(8,128)} slice(s32[1024,2047]{1,0:T(8,128)} %reshape.157), slice={[0:1024], [1023:2047]} | slice | bytes 8388608 | tf_op jit(solution)/shard_map/while/body/eval_jaxpr/slice | solution.py:22
  166.8 7.0 %fusion.4 = s32[1,2048]{1,0:T(1,128)S(1)} fusion(s32[1024,1]{0,1:T(1,128)S(1)} %bitcast.94, s32[1024,1024]{1,0:T(8,128)S(1)} %copy-done.3, s32[1024,1024]{1,0:T(8,128)S(1)} %copy-done.2), kind=kOutput, calls=%fused_computation.8 | convolution fusion | flops 6291456 | bytes 8400896 | tf_op jit(solution)/shard_map/while/body/eval_jaxpr/dot_general | solution.py:38
  173.8 6.8 %fusion = s32[1,2048]{1,0:T(1,128)S(1)} fusion(s32[1024,1]{0,1:T(1,128)S(1)} %bitcast.93, s32[1024,1024]{1,0:T(8,128)S(1)} %copy-done.7, s32[1024,1024]{1,0:T(8,128)S(1)} %copy-done.4), kind=kOutput, calls=%fused_computation.4 | convolution fusion | flops 6291456 | bytes 8400896 | tf_op jit(solution)/shard_map/while/body/eval_jaxpr/dot_general | solution.py:38
  188.5 12.3 %reshape.162 = s32[1024,2047]{1,0:T(8,128)} reshape(s32[2096128]{0:T(1024)} %slice.313) | data formatting | bytes 16769024 | tf_op jit(solution)/shard_map/while/body/eval_jaxpr/reshape | solution.py:22
  200.8 5.5 %slice.314 = s32[1024,1024]{1,0:T(8,128)} slice(s32[1024,2047]{1,0:T(8,128)} %reshape.162), slice={[0:1024], [1023:2047]} | slice | bytes 8388608 | tf_op jit(solution)/shard_map/while/body/eval_jaxpr/slice | solution.py:22
  206.4 5.4 %copy.13 = s32[128,16,8,128]{3,1,2,0:T(8,128)S(1)} copy(s32[128,16,8,128]{3,2,1,0:T(8,128)} %broadcast_bitcast_fusion) | data formatting | bytes 16777216
  215.4 12.3 %reshape.163 = s32[1024,2047]{1,0:T(8,128)} reshape(s32[2096128]{0:T(1024)} %slice.318) | data formatting | bytes 16769024 | tf_op jit(solution)/shard_map/while/body/eval_jaxpr/reshape | solution.py:22
  227.8 5.5 %slice.319 = s32[1024,1024]{1,0:T(8,128)} slice(s32[1024,2047]{1,0:T(8,128)} %reshape.163), slice={[0:1024], [1023:2047]} | slice | bytes 8388608 | tf_op jit(solution)/shard_map/while/body/eval_jaxpr/slice | solution.py:22
  233.2 5.4 %copy.10 = s32[128,16,8,128]{3,1,2,0:T(8,128)S(1)} copy(s32[128,16,8,128]{3,2,1,0:T(8,128)} %broadcast_bitcast_fusion.3) | data formatting | bytes 16777216
  242.3 12.3 %reshape.160 = s32[1024,2047]{1,0:T(8,128)} reshape(s32[2096128]{0:T(1024)} %slice.303) | data formatting | bytes 16769024 | tf_op jit(solution)/shard_map/while/body/eval_jaxpr/reshape | solution.py:22
  254.6 5.4 %slice.304 = s32[1024,1024]{1,0:T(8,128)} slice(s32[1024,2047]{1,0:T(8,128)} %reshape.160), slice={[0:1024], [1023:2047]} | slice | bytes 8388608 | tf_op jit(solution)/shard_map/while/body/eval_jaxpr/slice | solution.py:22
  260.0 5.4 %copy.11 = s32[128,16,8,128]{3,1,2,0:T(8,128)S(1)} copy(s32[128,16,8,128]{3,2,1,0:T(8,128)} %broadcast_bitcast_fusion.2) | data formatting | bytes 16777216
  269.2 12.3 %reshape.161 = s32[1024,2047]{1,0:T(8,128)} reshape(s32[2096128]{0:T(1024)} %slice.308) | data formatting | bytes 16769024 | tf_op jit(solution)/shard_map/while/body/eval_jaxpr/reshape | solution.py:22
  281.5 5.4 %slice.309 = s32[1024,1024]{1,0:T(8,128)} slice(s32[1024,2047]{1,0:T(8,128)} %reshape.161), slice={[0:1024], [1023:2047]} | slice | bytes 8388608 | tf_op jit(solution)/shard_map/while/body/eval_jaxpr/slice | solution.py:22
  301.6 9.5 %fusion.12 = s32[1,2048]{1,0:T(1,128)S(1)} fusion(s32[1024,1]{0,1:T(1,128)S(1)} %bitcast.96, s32[1024,1024]{1,0:T(8,128)} %slice.319, s32[1024,1024]{1,0:T(8,128)} %slice.314), kind=kOutput, calls=%fused_computation.16 | convolution fusion | flops 6291456 | bytes 8400896 | tf_op jit(solution)/shard_map/while/body/eval_jaxpr/dot_general | solution.py:38
  311.1 6.8 %fusion.8 = s32[1,2048]{1,0:T(1,128)S(1)} fusion(s32[1024,1]{0,1:T(1,128)S(1)} %bitcast.95, s32[1024,1024]{1,0:T(8,128)S(1)} %copy-done.6, s32[1024,1024]{1,0:T(8,128)S(1)} %copy-done.5), kind=kOutput, calls=%fused_computation.12 | convolution fusion | flops 6291456 | bytes 8400896 | tf_op jit(solution)/shard_map/while/body/eval_jaxpr/dot_general | solution.py:38
  (82 shorter events, 89.5 us)
Async XLA Ops:
  6.5 0.9 copy-start
  6.5 280.4 %all-reduce.3.cloned.1.call-start = ((), (), s32[]{:S(2)}) async-start(), calls=%async_computation | async-start | bytes 262144 | tf_op jit(solution)/shard_map/psum | solution.py:74
  83.9 5.5 %copy-start.8 = (s32[2,1024]{1,0:T(2,128)S(1)}, s32[2,1024]{1,0:T(2,128)}, u32[]{:S(2)}) copy-start(s32[2,1024]{1,0:T(2,128)} %param.10) | copy-start | bytes 24580
  160.3 5.3 %copy-start.2 = (s32[1024,1024]{1,0:T(8,128)S(1)}, s32[1024,1024]{1,0:T(8,128)}, u32[]{:S(2)}) copy-start(s32[1024,1024]{1,0:T(8,128)} %slice.293) | copy-start | bytes 12582916
  160.3 6.5 %copy-start.3 = (s32[1024,1024]{1,0:T(8,128)S(1)}, s32[1024,1024]{1,0:T(8,128)}, u32[]{:S(2)}) copy-start(s32[1024,1024]{1,0:T(8,128)} %slice.298) | copy-start | bytes 12582916
  160.3 13.5 %copy-start.4 = (s32[1024,1024]{1,0:T(8,128)S(1)}, s32[1024,1024]{1,0:T(8,128)}, u32[]{:S(2)}) copy-start(s32[1024,1024]{1,0:T(8,128)} %slice.283) | copy-start | bytes 12582916
  160.3 13.5 %copy-start.7 = (s32[1024,1024]{1,0:T(8,128)S(1)}, s32[1024,1024]{1,0:T(8,128)}, u32[]{:S(2)}) copy-start(s32[1024,1024]{1,0:T(8,128)} %slice.288) | copy-start | bytes 12582916
  166.8 15.7 %slice-start = ((s8[8388608]{0:T(1024)(128)(4,1)}), s8[4194304]{0:T(1024)(128)(4,1)S(1)}, s32[]{:S(2)}) async-start(s8[8388608]{0:T(1024)(128)(4,1)} %bitcast.78), calls=%async_computation.1 | async-start | bytes 8388608
  173.8 8.7 %slice-start.1 = ((s8[8388608]{0:T(1024)(128)(4,1)}), s8[4194304]{0:T(1024)(128)(4,1)S(1)}, s32[]{:S(2)}) async-start(s8[8388608]{0:T(1024)(128)(4,1)} %bitcast.78), calls=%async_computation.2 | async-start | bytes 8388608
  301.5 9.6 %copy-start.5 = (s32[1024,1024]{1,0:T(8,128)S(1)}, s32[1024,1024]{1,0:T(8,128)}, u32[]{:S(2)}) copy-start(s32[1024,1024]{1,0:T(8,128)} %slice.304) | copy-start | bytes 12582916
  301.6 9.6 %copy-start.6 = (s32[1024,1024]{1,0:T(8,128)S(1)}, s32[1024,1024]{1,0:T(8,128)}, u32[]{:S(2)}) copy-start(s32[1024,1024]{1,0:T(8,128)} %slice.309) | copy-start | bytes 12582916
  301.6 17.0 %copy-start.1 = (s32[16,2048]{1,0:T(8,128)S(1)}, s32[16,2048]{1,0:T(8,128)}, u32[]{:S(2)}) copy-start(s32[16,2048]{1,0:T(8,128)} %param.7) | copy-start | bytes 393220
Sparse Core Ops, SparseCore 0:
  10.9 91.1 all-reduce.2
